TPU v7x, 256 devices: a whole 4x4x8 slice. The times are simulated.
256 devices in a mesh: blk: 32 (over z, y_hi, core), cls: 8 (over x, y_lo).
Axes of the slice: x: 4, y: 4 (y_hi: 2, y_lo: 2; y = y_hi * 2 + y_lo), z: 8, core: 2. Of those that a mesh axis runs over, the one named last changes fastest.
Arguments:
- features: bfloat16 [2048, 2048], P('blk'), may hold values from -6 to 6
- labels: int32 [2048], P('blk'), may hold values from 0 to 655359
- offset: int32 [1], replicated, may hold values from 0 to 524288
- other_lse: float32 [2048], replicated, may hold values from 15 to 20
- weight: bfloat16 [131072, 2048], P(('blk', 'cls'))
- accum: float32 [131072, 2048], P(('blk', 'cls')), may hold values from 0.1 to 1
Outputs:
- new_weight: bfloat16 [131072, 2048], P(('blk', 'cls'))
- new_accum: float32 [131072, 2048], P(('blk', 'cls'))
- lse: float32 [2048], P('blk')
All inputs are finite; a program needn't handle non-finite values.
Results may differ from a plain program's by a relative error of at most 0.004.
Values may be sent and summed in bfloat16 or wider, within the bound.
A program may use at most 128 MiB of HBM per device.

v0:
```python
import jax
import jax.numpy as jnp
from jax import lax
from jax.sharding import PartitionSpec as P


def scores(rows, weight):
    return lax.dot_general(
        rows, weight, (((1,), (1,)), ((), ())), preferred_element_type=jnp.float32
    )


def gradient_term(logits, lse_rows, label_rows, first_class, rows):
    width = logits.shape[1]
    local = label_rows - first_class
    onehot = (local[:, None] == jnp.arange(width, dtype=jnp.int32)[None, :]).astype(jnp.float32)
    delta = (jnp.exp(logits - lse_rows[:, None]) - onehot).astype(jnp.bfloat16)
    return lax.dot_general(
        delta, rows, (((0,), (0,)), ((), ())), preferred_element_type=jnp.float32
    )


def body(features, labels, offset, other_lse, weight, accum):
    block = features.shape[0]
    cls_dev = weight.shape[0]
    device_rank = lax.axis_index("blk") * lax.axis_size("cls") + lax.axis_index("cls")
    first_class = offset[0] + device_rank * cls_dev
    all_rows, all_labels = (
        lax.all_gather(features, "blk", axis=0, tiled=True),
        lax.all_gather(labels, "blk", axis=0, tiled=True),
    )
    logits = scores(all_rows, weight)
    local_top = jnp.max(logits, axis=1)
    top = lax.pmax(local_top, ("blk", "cls"))
    total = lax.psum(jnp.sum(jnp.exp(logits - top[:, None]), axis=1), ("blk", "cls"))
    slab_lse = top + jnp.log(total)
    high = jnp.maximum(slab_lse, other_lse)
    lse = high + jnp.log(jnp.exp(slab_lse - high) + jnp.exp(other_lse - high))
    grad = gradient_term(logits, lse, all_labels, first_class, all_rows)
    new_accum = accum + grad * grad
    new_weight = (weight.astype(jnp.float32) - 0.05 * grad / (jnp.sqrt(new_accum) + 1e-10)).astype(
        jnp.bfloat16
    )
    own_lse = lax.dynamic_slice_in_dim(lse, lax.axis_index("blk") * block, block, 0)
    return (new_weight, new_accum, own_lse)


def solution(mesh):
    in_specs = (
        P("blk", None),
        P("blk"),
        P(),
        P(),
        P(("blk", "cls"), None),
        P(("blk", "cls"), None),
    )
    out_specs = (P(("blk", "cls"), None), P(("blk", "cls"), None), P("blk"))
    return jax.shard_map(body, mesh=mesh, in_specs=in_specs, out_specs=out_specs, check_vma=False)
```

profile of v0, /device:TPU:1, one launch (start us, length us, event | category | flops | bytes accessed | tf_op | source)
XLA Modules:
  0.0 299.9 jit_solution(17665709030679258281)
XLA Ops:
  7.2 0.0 all-gather.2.cloned.1.call-start
  7.2 0.7 all-gather.2.cloned.1.call-update
  8.6 1.3 dynamic-slice
  10.5 0.9 dynamic-update-slice
  11.4 18.9 %all-reduce = s32[2048]{0:T(1024)S(1)} all-reduce(s32[2048]{0:T(1024)S(1)} %dynamic-update-slice), channel_id=1, replica_groups=mesh['blk'=32,'cls'=8] {'blk'}, use_global_device_ids=true, to_apply=%add | all-reduce | flops 2048 | bytes 16384
  30.2 86.2 %all-gather.2.cloned.1.call-done = bf16[2048,2048]{1,0:T(8,128)(2,1)} async-done(((bf16[64,2048]{1,0:T(8,128)(2,1)}), bf16[2048,2048]{1,0:T(8,128)(2,1)}) %all-gather.2.cloned.1.call-update) | async-done | bytes 8388624 | tf_op jit(solution)/shard_map/all_gather | solution.py:29
  116.5 10.5 %fusion.4 = (f32[2048]{0:T(1024)S(1)}, f32[2048,512]{0,1:T(8,128)}) fusion(bf16[2048,2048]{1,0:T(8,128)(2,1)} %all-gather.2.cloned.1.call-done, bf16[512,2048]{1,0:T(8,128)(2,1)} %param.10), kind=kOutput, calls=%fused_computation.12 | convolution fusion | flops 4296013824 | bytes 14688256 | tf_op jit(solution)/shard_map/dot_general | solution.py:8
  127.0 0.0 copy-start
  127.0 0.0 copy-start.1
  127.0 74.8 %pmax.7 = f32[2048]{0:T(1024)S(1)} all-reduce(f32[2048]{0:T(1024)S(1)} %get-tuple-element.5), channel_id=1, replica_groups=mesh['blk'=32,'cls'=8] {'blk','cls'}, use_global_device_ids=true, to_apply=%region_1.0 | all-reduce | flops 2048 | bytes 16384 | tf_op jit(solution)/shard_map/pmax | solution.py:34
  201.8 2.8 exponential_reduce_fusion
  204.5 73.3 %psum.7 = f32[2048]{0:T(1024)S(1)} all-reduce(f32[2048]{0:T(1024)S(1)} %exponential_reduce_fusion), channel_id=1, replica_groups=mesh['blk'=32,'cls'=8] {'blk','cls'}, use_global_device_ids=true, to_apply=%region_3.0 | all-reduce | flops 2048 | bytes 16384 | tf_op jit(solution)/shard_map/psum | solution.py:35
  277.8 0.0 copy-done
  277.9 0.6 dynamic_slice.3
  278.5 0.0 copy-done.1
  278.5 14.6 %subtract_convert_fusion = (bf16[512,2048]{1,0:T(8,128)(2,1)}, f32[512,2048]{1,0:T(8,128)}) fusion(bf16[512,2048]{1,0:T(8,128)(2,1)S(1)} %copy-done.1, f32[512,2048]{1,0:T(8,128)} %param.11, bf16[2048,2048]{1,0:T(8,128)(2,1)} %all-gather.2.cloned.1.call-done, f32[2048,512]{0,1:T(8,128)} %get-tuple-element.6, s32[2048]{0:T(1024)S(1)} %broadcast_subtract_fusion, ...), kind=kOutput, calls=%fused_computation | convolution fusion | flops 4308598784 | bytes 25182208 | tf_op jit(solution)/shard_map/dot_general | solution.py:18
  (3 shorter events, 0.0 us)
Async XLA Ops:
  7.2 109.3 %all-gather.2.cloned.1.call-start = ((), (), s32[]{:S(2)}) async-start(), calls=%async_computation | async-start | bytes 8650752 | tf_op jit(solution)/shard_map/all_gather | solution.py:29
  127.0 150.9 %copy-start = (f32[2048]{0:T(1024)S(1)}, f32[2048]{0:T(1024)}, u32[]{:S(2)}) copy-start(f32[2048]{0:T(1024)} %param.9) | copy-start | bytes 24580
  127.0 151.5 %copy-start.1 = (bf16[512,2048]{1,0:T(8,128)(2,1)S(1)}, bf16[512,2048]{1,0:T(8,128)(2,1)}, u32[]{:S(2)}) copy-start(bf16[512,2048]{1,0:T(8,128)(2,1)} %param.10) | copy-start | bytes 6291460
Sparse Core Ops, SparseCore 0:
  10.8 105.6 all-gather.1
where the time goes:
time: 300 us
  blocking collectives  167 us (56%)
  waiting for transfers between devices  86.9 us (29%)
  matrix products  25.1 us (8%)
  between operations  15.4 us (5%)
    all_gather x1, waiting for transfers between devices, body(): lax.all_gather(features, 'blk', axis=0, tiled=True)  86.2 us
    pmax x1, blocking collectives, body(): top = lax.pmax(local_top, ('blk', 'cls'))  74.8 us
    psum x1, blocking collectives, body(): lax.psum(jnp.sum(jnp.exp(logits - top[:, None]), axis=1), ('blk', 'cls'))  73.3 us
    unnamed x1, blocking collectives  18.9 us
    dot_general x1, matrix products, gradient_term(): lax.dot_general(delta, rows, (((0,), (0,)), ((), ())), preferred_element_...  14.6 us
    dot_general x1, matrix products, scores(): lax.dot_general(rows, weight, (((1,), (1,)), ((), ())), preferred_element...  10.5 us
  transfers between devices with their start and end apart: 1, of which 1 were waited for; matrix products, arithmetic and copies ran while one was open for 1% of the time, Pallas kernels for 0%

commit v1 on v0

--- a/solution.py
+++ b/solution.py
@@ -32,7 +32,9 @@
     logits = scores(all_rows, weight)
     local_top = jnp.max(logits, axis=1)
     top = lax.pmax(local_top, ("blk", "cls"))
-    total = lax.psum(jnp.sum(jnp.exp(logits - top[:, None]), axis=1), ("blk", "cls"))
+    total = jnp.sum(
+        lax.all_gather(jnp.sum(jnp.exp(logits - top[:, None]), axis=1), ("blk", "cls")), axis=0
+    )
     slab_lse = top + jnp.log(total)
     high = jnp.maximum(slab_lse, other_lse)
     lse = high + jnp.log(jnp.exp(slab_lse - high) + jnp.exp(other_lse - high))

time: 300 us -> 923 us (3.08)
  waiting for transfers between devices: 86.9 us -> 786 us
  blocking collectives: 167 us -> 86.8 us
    all_gather x0 -> x1, waiting for transfers between devices: none -> 677 us  [body(): lax.all_gather(jnp.sum(jnp.exp(logits - top[:, None]), axis=1), ('blk', '...]
    psum x1 -> x0, blocking collectives: 73.3 us -> none  [body(): lax.psum(jnp.sum(jnp.exp(logits - top[:, None]), axis=1), ('blk', 'cls'))]
    all_gather x1, waiting for transfers between devices: 86.2 us -> 109 us  [body(): lax.all_gather(features, 'blk', axis=0, tiled=True)]
  transfers between devices with their start and end apart: 1 -> 2, of which waited for: 1 -> 2; matrix products, arithmetic and copies ran while one was open for 1% -> 0% of each run, Pallas kernels for 0% -> 0%
where the time goes in v1:
time: 923 us; the launch traced here: 921 us
  waiting for transfers between devices  786 us (85%)
  blocking collectives  86.8 us (9%)
  matrix products  25.6 us (3%)
  between operations  15.4 us (2%)
    all_gather x1, waiting for transfers between devices, body(): lax.all_gather(jnp.sum(jnp.exp(logits - top[:, None]), axis=1), ('blk', '...  677 us
    all_gather x1, waiting for transfers between devices, body(): lax.all_gather(features, 'blk', axis=0, tiled=True)  109 us
    pmax x1, blocking collectives, body(): top = lax.pmax(local_top, ('blk', 'cls'))  74.8 us
  transfers between devices with their start and end apart: 2, of which 2 were waited for; matrix products, arithmetic and copies ran while one was open for 0% of the time, Pallas kernels for 0%

profile of v1, /device:TPU:1, one launch (start us, length us, event | category | flops | bytes accessed | tf_op | source)
XLA Modules:
  0.0 920.6 jit_solution(5326063140376025625)
XLA Ops:
  7.2 0.0 all-gather.4.cloned.1.call-start
  7.2 0.7 all-gather.4.cloned.1.call-update
  7.9 0.0 all-gather.6.cloned.1.call-start
  7.9 108.5 %all-gather.4.cloned.1.call-done = bf16[2048,2048]{1,0:T(8,128)(2,1)} async-done(((bf16[64,2048]{1,0:T(8,128)(2,1)}), bf16[2048,2048]{1,0:T(8,128)(2,1)}) %all-gather.4.cloned.1.call-update) | async-done | bytes 8388624 | tf_op jit(solution)/shard_map/all_gather | solution.py:29
  116.5 10.5 %fusion.4 = (f32[2048]{0:T(1024)S(1)}, f32[2048,512]{0,1:T(8,128)}) fusion(bf16[2048,2048]{1,0:T(8,128)(2,1)} %all-gather.4.cloned.1.call-done, bf16[512,2048]{1,0:T(8,128)(2,1)} %param.10), kind=kOutput, calls=%fused_computation.12 | convolution fusion | flops 4296013824 | bytes 14688256 | tf_op jit(solution)/shard_map/dot_general | solution.py:8
  127.0 0.0 copy-start.2
  127.0 0.0 copy-start.1
  127.0 74.8 %pmax.7 = f32[2048]{0:T(1024)S(1)} all-reduce(f32[2048]{0:T(1024)S(1)} %get-tuple-element.5), channel_id=1, replica_groups=mesh['blk'=32,'cls'=8] {'blk','cls'}, use_global_device_ids=true, to_apply=%region_1.0 | all-reduce | flops 2048 | bytes 16384 | tf_op jit(solution)/shard_map/pmax | solution.py:34
  201.7 3.4 exponential_reduce_fusion
  205.1 0.0 copy-start
  205.1 0.0 all-gather.6.cloned.1.call-update
  205.8 0.0 copy-done.2
  205.8 0.6 dynamic-slice
  207.1 0.0 copy-done.1
  207.1 0.3 dynamic-update-slice
  207.3 12.0 %all-reduce = s32[2048]{0:T(1024)S(1)} all-reduce(s32[2048]{0:T(1024)S(1)} %dynamic-update-slice), channel_id=1, replica_groups=mesh['blk'=32,'cls'=8] {'blk'}, use_global_device_ids=true, to_apply=%add | all-reduce | flops 2048 | bytes 16384
  219.4 676.7 %all-gather.6.cloned.1.call-done = f32[524288]{0:T(1024)} async-done(((f32[2048]{0:T(1024)}), f32[524288]{0:T(1024)}) %all-gather.6.cloned.1.call-update) | async-done | bytes 2097168 | tf_op jit(solution)/shard_map/all_gather | solution.py:36
  896.1 1.7 reshape.9
  897.9 0.1 reduce_sum.19
  898.0 0.0 copy-done
  898.0 0.6 dynamic_slice.3
  898.6 15.2 %subtract_convert_fusion = (bf16[512,2048]{1,0:T(8,128)(2,1)}, f32[512,2048]{1,0:T(8,128)}) fusion(bf16[512,2048]{1,0:T(8,128)(2,1)} %param.10, f32[512,2048]{1,0:T(8,128)} %param.11, bf16[2048,2048]{1,0:T(8,128)(2,1)} %all-gather.4.cloned.1.call-done, f32[2048,512]{0,1:T(8,128)} %get-tuple-element.6, s32[2048]{0:T(1024)S(1)} %broadcast_subtract_fusion, ...), kind=kOutput, calls=%fused_computation | convolution fusion | flops 4308598784 | bytes 25182208 | tf_op jit(solution)/shard_map/dot_general | solution.py:18
  (3 shorter events, 0.0 us)
Async XLA Ops:
  7.2 109.3 %all-gather.4.cloned.1.call-start = ((), (), s32[]{:S(2)}) async-start(), calls=%async_computation | async-start | bytes 8650752 | tf_op jit(solution)/shard_map/all_gather | solution.py:29
  7.9 888.3 %all-gather.6.cloned.1.call-start = ((), (), s32[]{:S(2)}) async-start(), calls=%async_computation.1 | async-start | bytes 2105344 | tf_op jit(solution)/shard_map/all_gather | solution.py:36
  127.0 78.8 %copy-start.2 = (u32[256]{0:T(256)S(1)}, u32[256]{0:T(256)}, u32[]{:S(2)}) copy-start(u32[256]{0:T(256)} %constant.29) | copy-start | bytes 3076
  127.0 80.1 %copy-start.1 = (s32[64]{0:T(128)S(1)}, s32[64]{0:T(128)}, u32[]{:S(2)}) copy-start(s32[64]{0:T(128)} %param.7) | copy-start | bytes 772
  205.1 692.9 %copy-start = (f32[2048]{0:T(1024)S(1)}, f32[2048]{0:T(1024)}, u32[]{:S(2)}) copy-start(f32[2048]{0:T(1024)} %param.9) | copy-start | bytes 24580
Sparse Core Ops, SparseCore 0:
  10.8 105.6 all-gather.3
  205.3 690.8 all-gather.5

commit v2 on v0

--- a/solution.py
+++ b/solution.py
@@ -32,7 +32,7 @@
     logits = scores(all_rows, weight)
     local_top = jnp.max(logits, axis=1)
     top = lax.pmax(local_top, ("blk", "cls"))
-    total = lax.psum(jnp.sum(jnp.exp(logits - top[:, None]), axis=1), ("blk", "cls"))
+    total = lax.psum(lax.psum(jnp.sum(jnp.exp(logits - top[:, None]), axis=1), "cls"), "blk")
     slab_lse = top + jnp.log(total)
     high = jnp.maximum(slab_lse, other_lse)
     lse = high + jnp.log(jnp.exp(slab_lse - high) + jnp.exp(other_lse - high))

time: 300 us -> 311 us (1.037)
  blocking collectives: 167 us -> 177 us
    psum x1 -> x2, blocking collectives: 73.3 us -> 83.8 us  [the longest x1 69.8 us: body(): lax.psum(lax.psum(jnp.sum(jnp.exp(logits - top[:, None]), axis=1), 'cls')...]
where the time goes in v2:
time: 311 us; the launch traced here: 310 us
  blocking collectives  177 us (57%)
  waiting for transfers between devices  86.9 us (28%)
  matrix products  25.1 us (8%)
  between operations  15.4 us (5%)
    all_gather x1, waiting for transfers between devices, body(): lax.all_gather(features, 'blk', axis=0, tiled=True)  86.2 us
    pmax x1, blocking collectives, body(): top = lax.pmax(local_top, ('blk', 'cls'))  74.8 us
    psum x1, blocking collectives, body(): lax.psum(lax.psum(jnp.sum(jnp.exp(logits - top[:, None]), axis=1), 'cls')...  69.8 us
    unnamed x1, blocking collectives  18.9 us
    dot_general x1, matrix products, gradient_term(): lax.dot_general(delta, rows, (((0,), (0,)), ((), ())), preferred_element_...  14.6 us
    psum x1, blocking collectives, body(): lax.psum(jnp.sum(jnp.exp(logits - top[:, None]), axis=1), 'cls')  14 us
    dot_general x1, matrix products, scores(): lax.dot_general(rows, weight, (((1,), (1,)), ((), ())), preferred_element...  10.5 us
  transfers between devices with their start and end apart: 1, of which 1 were waited for; matrix products, arithmetic and copies ran while one was open for 1% of the time, Pallas kernels for 0%

profile of v2, /device:TPU:1, one launch (start us, length us, event | category | flops | bytes accessed | tf_op | source)
XLA Modules:
  0.0 310.4 jit_solution(328261019161317494)
XLA Ops:
  7.2 0.0 all-gather.2.cloned.1.call-start
  7.2 0.7 all-gather.2.cloned.1.call-update
  8.6 1.3 dynamic-slice
  10.5 0.9 dynamic-update-slice
  11.4 18.9 %all-reduce = s32[2048]{0:T(1024)S(1)} all-reduce(s32[2048]{0:T(1024)S(1)} %dynamic-update-slice), channel_id=1, replica_groups=mesh['blk'=32,'cls'=8] {'blk'}, use_global_device_ids=true, to_apply=%add | all-reduce | flops 2048 | bytes 16384
  30.2 86.2 %all-gather.2.cloned.1.call-done = bf16[2048,2048]{1,0:T(8,128)(2,1)} async-done(((bf16[64,2048]{1,0:T(8,128)(2,1)}), bf16[2048,2048]{1,0:T(8,128)(2,1)}) %all-gather.2.cloned.1.call-update) | async-done | bytes 8388624 | tf_op jit(solution)/shard_map/all_gather | solution.py:29
  116.5 10.5 %fusion.4 = (f32[2048]{0:T(1024)S(1)}, f32[2048,512]{0,1:T(8,128)}) fusion(bf16[2048,2048]{1,0:T(8,128)(2,1)} %all-gather.2.cloned.1.call-done, bf16[512,2048]{1,0:T(8,128)(2,1)} %param.10), kind=kOutput, calls=%fused_computation.12 | convolution fusion | flops 4296013824 | bytes 14688256 | tf_op jit(solution)/shard_map/dot_general | solution.py:8
  127.0 0.0 copy-start
  127.0 0.0 copy-start.1
  127.0 74.8 %pmax.7 = f32[2048]{0:T(1024)S(1)} all-reduce(f32[2048]{0:T(1024)S(1)} %get-tuple-element.5), channel_id=1, replica_groups=mesh['blk'=32,'cls'=8] {'blk','cls'}, use_global_device_ids=true, to_apply=%region_1.0 | all-reduce | flops 2048 | bytes 16384 | tf_op jit(solution)/shard_map/pmax | solution.py:34
  201.8 2.8 exponential_reduce_fusion
  204.5 14.0 %psum.14 = f32[2048]{0:T(1024)S(1)} all-reduce(f32[2048]{0:T(1024)S(1)} %exponential_reduce_fusion), channel_id=1, replica_groups=mesh['blk'=32,'cls'=8] {'cls'}, use_global_device_ids=true, to_apply=%region_3.0 | all-reduce | flops 2048 | bytes 16384 | tf_op jit(solution)/shard_map/psum | solution.py:35
  218.5 69.8 %psum.15 = f32[2048]{0:T(1024)S(1)} all-reduce(f32[2048]{0:T(1024)S(1)} %psum.14), channel_id=1, replica_groups=mesh['blk'=32,'cls'=8] {'blk'}, use_global_device_ids=true, to_apply=%region_4.0 | all-reduce | flops 2048 | bytes 16384 | tf_op jit(solution)/shard_map/psum | solution.py:35
  288.3 0.0 copy-done
  288.4 0.6 dynamic_slice.3
  289.0 0.0 copy-done.1
  289.0 14.6 %subtract_convert_fusion = (bf16[512,2048]{1,0:T(8,128)(2,1)}, f32[512,2048]{1,0:T(8,128)}) fusion(bf16[512,2048]{1,0:T(8,128)(2,1)S(1)} %copy-done.1, f32[512,2048]{1,0:T(8,128)} %param.11, bf16[2048,2048]{1,0:T(8,128)(2,1)} %all-gather.2.cloned.1.call-done, f32[2048,512]{0,1:T(8,128)} %get-tuple-element.6, s32[2048]{0:T(1024)S(1)} %broadcast_subtract_fusion, ...), kind=kOutput, calls=%fused_computation | convolution fusion | flops 4308598784 | bytes 25182208 | tf_op jit(solution)/shard_map/dot_general | solution.py:18
  (3 shorter events, 0.0 us)
Async XLA Ops:
  7.2 109.3 %all-gather.2.cloned.1.call-start = ((), (), s32[]{:S(2)}) async-start(), calls=%async_computation | async-start | bytes 8650752 | tf_op jit(solution)/shard_map/all_gather | solution.py:29
  127.0 161.4 %copy-start = (f32[2048]{0:T(1024)S(1)}, f32[2048]{0:T(1024)}, u32[]{:S(2)}) copy-start(f32[2048]{0:T(1024)} %param.9) | copy-start | bytes 24580
  127.0 162.0 %copy-start.1 = (bf16[512,2048]{1,0:T(8,128)(2,1)S(1)}, bf16[512,2048]{1,0:T(8,128)(2,1)}, u32[]{:S(2)}) copy-start(bf16[512,2048]{1,0:T(8,128)(2,1)} %param.10) | copy-start | bytes 6291460
Sparse Core Ops, SparseCore 0:
  10.8 105.6 all-gather.1

commit v3 on v0

--- a/solution.py
+++ b/solution.py
@@ -26,7 +26,9 @@
     device_rank = lax.axis_index("blk") * lax.axis_size("cls") + lax.axis_index("cls")
     first_class = offset[0] + device_rank * cls_dev
     all_rows, all_labels = (
-        lax.all_gather(features, "blk", axis=0, tiled=True),
+        jnp.concatenate(
+            lax.all_to_all(jnp.stack([features] * lax.axis_size("blk")), "blk", 0, 0), axis=0
+        ),
         lax.all_gather(labels, "blk", axis=0, tiled=True),
     )
     logits = scores(all_rows, weight)

time: 300 us -> 386 us (1.29)
  blocking collectives: 167 us -> 337 us
  waiting for transfers between devices: 86.9 us -> 0.01 us
  between operations: 15.4 us -> 2.01 us
  starting transfers between devices: 0.04 us -> 12.9 us
  local copies, waits for them, and re-layouts: 2.74 us -> 6.69 us
    unnamed x1, blocking collectives: 18.9 us -> 185 us
    all_gather x1 -> x0, waiting for transfers between devices: 86.2 us -> none  [body(): lax.all_gather(features, 'blk', axis=0, tiled=True)]
    all_to_all x0 -> x1, starting transfers between devices: none -> 12.9 us  [body(): lax.all_to_all(jnp.stack([features] * lax.axis_size('blk')), 'blk', 0, 0)]
    another operation x0 -> x1, local copies, waits for them, and re-layouts: none -> 5.22 us  [body(): jnp.stack([features] * lax.axis_size('blk'))]
  transfers between devices with their start and end apart: 1 -> 1, of which waited for: 1 -> 0; matrix products, arithmetic and copies ran while one was open for 1% -> 0% of each run, Pallas kernels for 0% -> 0%
where the time goes in v3:
time: 386 us; the launch traced here: 385 us
  blocking collectives  337 us (87%)
  matrix products  24 us (6%)
  starting transfers between devices  12.9 us (3%)
  local copies, waits for them, and re-layouts  6.69 us (2%)
    unnamed x1, blocking collectives  185 us
    pmax x1, blocking collectives, body(): top = lax.pmax(local_top, ('blk', 'cls'))  78.5 us
    psum x1, blocking collectives, body(): lax.psum(jnp.sum(jnp.exp(logits - top[:, None]), axis=1), ('blk', 'cls'))  73.4 us
    dot_general x1, matrix products, gradient_term(): lax.dot_general(delta, rows, (((0,), (0,)), ((), ())), preferred_element_...  14.6 us
    all_to_all x1, starting transfers between devices, body(): lax.all_to_all(jnp.stack([features] * lax.axis_size('blk')), 'blk', 0, 0)  12.9 us
    dot_general x1, matrix products, scores(): lax.dot_general(rows, weight, (((1,), (1,)), ((), ())), preferred_element...  9.45 us
  transfers between devices with their start and end apart: 1, of which 0 were waited for; matrix products, arithmetic and copies ran while one was open for 0% of the time, Pallas kernels for 0%

profile of v3, /device:TPU:1, one launch (start us, length us, event | category | flops | bytes accessed | tf_op | source)
XLA Modules:
  0.0 385.5 jit_solution(2320218505429204021)
XLA Ops:
  0.6 5.2 %stack.2 = bf16[32,64,2048]{2,1,0:T(8,128)(2,1)} broadcast(bf16[64,2048]{1,0:T(8,128)(2,1)} %param.6), dimensions={1,2} | broadcast | bytes 8650752 | tf_op jit(solution)/shard_map/stack | solution.py:30
  5.9 0.0 copy-start.3
  5.9 0.0 copy-start.2
  5.9 0.0 copy-start.1
  5.9 12.9 %all-to-all-start = ((bf16[32,64,2048]{2,1,0:T(8,128)(2,1)}), bf16[32,64,2048]{2,1,0:T(8,128)(2,1)}, u32[]{:S(2)}, u32[]{:S(2)}) async-start(bf16[32,64,2048]{2,1,0:T(8,128)(2,1)} %stack.2), calls=%async_computation | async-start | bytes 16777216 | tf_op jit(solution)/shard_map/all_to_all | solution.py:30
  19.5 0.0 copy-done.3
  19.5 0.6 dynamic-slice
  20.7 0.0 copy-done.2
  20.7 0.3 dynamic-update-slice
  21.0 185.1 %all-reduce = s32[2048]{0:T(1024)S(1)} all-reduce(s32[2048]{0:T(1024)S(1)} %dynamic-update-slice), channel_id=1, replica_groups=mesh['blk'=32,'cls'=8] {'blk'}, use_global_device_ids=true, to_apply=%add | all-reduce | flops 2048 | bytes 16384
  206.1 0.0 all-to-all-done
  206.1 0.0 copy-done.1
  206.1 9.5 %fusion.4 = (f32[2048]{0:T(1024)S(1)}, f32[2048,512]{0,1:T(8,128)}) fusion(bf16[2048,2048]{1,0:T(8,128)(2,1)} %bitcast, bf16[512,2048]{1,0:T(8,128)(2,1)S(1)} %copy-done.1), kind=kOutput, calls=%fused_computation.12 | convolution fusion | flops 4296013824 | bytes 14688256 | tf_op jit(solution)/shard_map/dot_general | solution.py:8
  215.6 0.0 copy-start
  215.6 78.5 %pmax.7 = f32[2048]{0:T(1024)S(1)} all-reduce(f32[2048]{0:T(1024)S(1)} %get-tuple-element.5), channel_id=1, replica_groups=mesh['blk'=32,'cls'=8] {'blk','cls'}, use_global_device_ids=true, to_apply=%region_1.0 | all-reduce | flops 2048 | bytes 16384 | tf_op jit(solution)/shard_map/pmax | solution.py:36
  294.1 2.8 exponential_reduce_fusion
  296.9 73.4 %psum.7 = f32[2048]{0:T(1024)S(1)} all-reduce(f32[2048]{0:T(1024)S(1)} %exponential_reduce_fusion), channel_id=1, replica_groups=mesh['blk'=32,'cls'=8] {'blk','cls'}, use_global_device_ids=true, to_apply=%region_3.0 | all-reduce | flops 2048 | bytes 16384 | tf_op jit(solution)/shard_map/psum | solution.py:37
  370.3 0.0 copy-done
  370.3 0.6 dynamic_slice.3
  370.9 14.6 %subtract_convert_fusion = (bf16[512,2048]{1,0:T(8,128)(2,1)}, f32[512,2048]{1,0:T(8,128)}) fusion(bf16[512,2048]{1,0:T(8,128)(2,1)S(1)} %copy-done.1, f32[512,2048]{1,0:T(8,128)} %param.11, bf16[2048,2048]{1,0:T(8,128)(2,1)} %bitcast, f32[2048,512]{0,1:T(8,128)} %get-tuple-element.6, s32[2048]{0:T(1024)S(1)} %broadcast_subtract_fusion, f32[2048]{0:T(1024)S(1)} %log_add_fusion), kind=kOutput, calls=%fused_computation | convolution fusion | flops 4308598784 | bytes 25182208 | tf_op jit(solution)/shard_map/dot_general | solution.py:18
  (3 shorter events, 0.0 us)
Async XLA Ops:
  5.9 13.6 %copy-start.3 = (u32[256]{0:T(256)S(1)}, u32[256]{0:T(256)}, u32[]{:S(2)}) copy-start(u32[256]{0:T(256)} %constant.29) | copy-start | bytes 3076
  5.9 14.9 %copy-start.2 = (s32[64]{0:T(128)S(1)}, s32[64]{0:T(128)}, u32[]{:S(2)}) copy-start(s32[64]{0:T(128)} %param.7) | copy-start | bytes 772
  5.9 200.3 %copy-start.1 = (bf16[512,2048]{1,0:T(8,128)(2,1)S(1)}, bf16[512,2048]{1,0:T(8,128)(2,1)}, u32[]{:S(2)}) copy-start(bf16[512,2048]{1,0:T(8,128)(2,1)} %param.10) | copy-start | bytes 6291460
  5.9 200.3 %all-to-all-start = ((bf16[32,64,2048]{2,1,0:T(8,128)(2,1)}), bf16[32,64,2048]{2,1,0:T(8,128)(2,1)}, u32[]{:S(2)}, u32[]{:S(2)}) async-start(bf16[32,64,2048]{2,1,0:T(8,128)(2,1)} %stack.2), calls=%async_computation | async-start | bytes 16777216 | tf_op jit(solution)/shard_map/all_to_all | solution.py:30
  215.6 154.7 %copy-start = (f32[2048]{0:T(1024)S(1)}, f32[2048]{0:T(1024)}, u32[]{:S(2)}) copy-start(f32[2048]{0:T(1024)} %param.9) | copy-start | bytes 24580
